TPU v7x, 512 devices: a whole 4x4x16 slice. The times are simulated.
512 devices in a mesh: space: 32 (over y, z_lo), chan: 16 (over x, z_hi, core).
Axes of the slice: x: 4, y: 4, z: 16 (z_hi: 2, z_lo: 8; z = z_hi * 8 + z_lo), core: 2. Of those that a mesh axis runs over, the one named last changes fastest.
Arguments:
- latent: bfloat16 [1, 32, 160, 512], P(None, 'space', None, 'chan'), may hold values from -12 to 12
- cache_mid: bfloat16 [2, 32, 160, 512], P(None, 'space', None, 'chan'), may hold values from -6 to 6
- norm1_gain: float32 [512], P('chan'), may hold values from 0.1 to 1.9
- norm1_bias: float32 [512], P('chan'), may hold values from -3 to 3
- conv1_weight: bfloat16 [3, 3, 3, 512, 512], P(None, None, None, 'chan'), may hold values from -0.0625 to 0.0625
- conv1_bias: float32 [512], P('chan'), may hold values from -2 to 2
- cache_up: bfloat16 [2, 64, 320, 512], P(None, 'space', 'chan'), may hold values from -6 to 6
- norm2_gain: float32 [512], replicated, may hold values from 0.1 to 1.9
- norm2_bias: float32 [512], replicated, may hold values from -3 to 3
- conv2_weight: bfloat16 [3, 3, 3, 512, 512], P(None, None, None, None, 'chan'), may hold values from -0.0546875 to 0.0546875
- conv2_bias: float32 [512], replicated, may hold values from -2 to 2
Outputs:
- up_features: bfloat16 [1, 64, 320, 512], P(None, 'space', 'chan')
All inputs are finite; a program needn't handle non-finite values.
Results may differ from a plain program's by a relative error of at most 0.0038.
The roundings to bfloat16 on the way count: a program that leaves them out, or rounds other values in their place, can miss the bound.
Values may be sent and summed in bfloat16 or wider, within the bound.
No kernel may reach another device: no remote copies, remote signals or barrier semaphores. Data moves between devices by JAX's collectives and lax.ppermute only.
A program may use at most 64 MiB of HBM per device.

v0:
```python
import jax
import jax.numpy as jnp
from jax import lax
from jax.sharding import PartitionSpec as P

GROUPS = 32
GS = 16
epsilon = 1e-06


def extended(cells, sides, width):
    for axis, dim in sides:
        count = lax.axis_size(axis)
        ends = count - 1
        head = lax.slice_in_dim(cells, 0, width, axis=dim)
        tail = lax.slice_in_dim(cells, cells.shape[dim] - width, cells.shape[dim], axis=dim)
        cells = jnp.concatenate(
            [
                lax.ppermute(tail, axis, [(i, (i + 1) % count) for i in range(ends)]),
                cells,
                lax.ppermute(head, axis, [((i + 1) % count, i) for i in range(ends)]),
            ],
            axis=dim,
        )
    return cells


def unfold(padded, frames, height, breadth):
    pieces = []
    for shift_time in range(3):
        for shift_row in range(3):
            for shift_col in range(3):
                pieces.append(
                    padded[
                        shift_time : shift_time + frames,
                        shift_row : shift_row + height,
                        shift_col : shift_col + breadth,
                        :,
                    ]
                )
    return jnp.concatenate(pieces, axis=-1)


def norm_apply(upsampled, mean_chan, scale_chan, gain, bias):
    scaled = (upsampled.astype(jnp.float32) - mean_chan) * scale_chan
    return jax.nn.silu(scaled * gain + bias).astype(jnp.bfloat16)


def on_device(
    latent,
    cache_mid,
    norm1_gain,
    norm1_bias,
    conv1_weight,
    conv1_bias,
    cache_up,
    norm2_gain,
    norm2_bias,
    conv2_weight,
    conv2_bias,
):
    frames, height, breadth, chan_here = latent.shape
    groups_here = chan_here // GS
    values = latent.astype(jnp.float32)
    grouped = values.reshape(frames, height, breadth, groups_here, GS)
    entries = frames * height * lax.axis_size("space") * breadth * GS
    group_mean = lax.psum(jnp.sum(grouped, axis=(0, 1, 2, 4)), "space") / entries
    centred = grouped - group_mean[:, None]
    group_var = lax.psum(jnp.sum(centred * centred, axis=(0, 1, 2, 4)), "space") / entries
    scaled = (centred * lax.rsqrt(group_var + epsilon)[:, None]).reshape(
        frames, height, breadth, chan_here
    )
    normed_mid = jax.nn.silu(scaled * norm1_gain + norm1_bias).astype(jnp.bfloat16)
    joined = jnp.concatenate([cache_mid, normed_mid], axis=0)
    rimmed = extended(joined, (("space", 1),), 1)
    padded = jnp.pad(rimmed, ((0, 0), (0, 0), (1, 1), (0, 0)))
    columns = unfold(padded, frames, height, breadth).reshape(frames * height * breadth, -1)
    kernel = conv1_weight.reshape(-1, conv1_weight.shape[-1])
    summed = lax.psum_scatter(
        lax.dot_general(
            kernel, columns, (((0,), (1,)), ((), ())), preferred_element_type=jnp.float32
        ),
        "chan",
        scatter_dimension=0,
        tiled=True,
    )
    conv_mid = summed.T.reshape(frames, height, breadth, chan_here)
    merged = (values + conv_mid + conv1_bias).astype(jnp.bfloat16)
    merged_groups = merged.astype(jnp.float32).reshape(frames, height, breadth, groups_here, GS)
    first_group = lax.axis_index("chan") * groups_here

    def place(partial_value):
        return lax.dynamic_update_slice_in_dim(
            jnp.zeros((GROUPS,), jnp.float32), partial_value, first_group, 0
        )

    own_sum = jnp.sum(merged_groups, axis=(0, 1, 2, 4))
    up_mean = lax.psum(place(own_sum), ("space", "chan")) / entries
    own_mean = lax.dynamic_slice_in_dim(up_mean, first_group, groups_here)
    deviation = merged_groups - own_mean[:, None]
    up_var = (
        lax.psum(place(jnp.sum(deviation * deviation, axis=(0, 1, 2, 4))), ("space", "chan"))
        / entries
    )
    mean_chan = jnp.repeat(up_mean, GS)
    scale_chan = jnp.repeat(lax.rsqrt(up_var + epsilon), GS)
    pixel_tile = lax.all_to_all(merged, "chan", split_axis=2, concat_axis=3, tiled=True)
    upsampled = jnp.repeat(jnp.repeat(pixel_tile, 2, axis=1), 2, axis=2)
    normed_up = norm_apply(upsampled, mean_chan, scale_chan, norm2_gain, norm2_bias)
    joined_up = jnp.concatenate([cache_up, normed_up], axis=0)
    rimmed_up = extended(joined_up, (("space", 1), ("chan", 2)), 1)
    up_height = normed_up.shape[1]
    up_breadth = normed_up.shape[2]
    up_columns = unfold(rimmed_up, frames, up_height, up_breadth).reshape(
        frames * up_height * up_breadth, -1
    )
    kernel_up = conv2_weight.reshape(-1, conv2_weight.shape[-1])
    up_conv = jnp.dot(
        up_columns,
        lax.all_gather(kernel_up, "chan", axis=1, tiled=True),
        preferred_element_type=jnp.float32,
    )
    result = (up_conv + conv2_bias).astype(jnp.bfloat16).reshape(frames, up_height, up_breadth, -1)
    return result


def solution(mesh):
    placed = (
        P(None, "space", None, "chan"),
        P(None, "space", None, "chan"),
        P("chan"),
        P("chan"),
        P(None, None, None, "chan", None),
        P("chan"),
        P(None, "space", "chan", None),
        P(),
        P(),
        P(None, None, None, None, "chan"),
        P(),
    )
    return jax.shard_map(
        on_device,
        mesh=mesh,
        in_specs=placed,
        out_specs=P(None, "space", "chan", None),
        check_vma=False,
    )
```

profile of v0, /device:TPU:480, one launch (start us, length us, event | category | flops | bytes accessed | tf_op | source)
XLA Modules:
  0.0 809.0 jit_solution(2814931638658902125)
XLA Ops:
  6.6 0.9 convert_reduce_fusion
  7.5 0.1 reduce_sum.47
  7.6 0.1 reduce_sum.51
  7.7 103.2 %psum.28 = f32[2]{0:T(128)S(1)} all-reduce(f32[2]{0:T(128)S(1)} %reduce_sum.51), channel_id=1, replica_groups=mesh['space'=32,'chan'=16] {'space'}, use_global_device_ids=true, to_apply=%region_2.0 | all-reduce | flops 2 | bytes 16 | tf_op jit(solution)/shard_map/psum | solution.py:67
  110.9 0.1 sub.57
  111.0 0.9 fusion.9
  111.9 0.1 reduce_sum.53
  112.0 0.1 reduce_sum.54
  112.1 105.8 %psum.29 = f32[2]{0:T(128)S(1)} all-reduce(f32[2]{0:T(128)S(1)} %reduce_sum.54), channel_id=1, replica_groups=mesh['space'=32,'chan'=16] {'space'}, use_global_device_ids=true, to_apply=%region_5.6 | all-reduce | flops 2 | bytes 16 | tf_op jit(solution)/shard_map/psum | solution.py:69
  218.0 0.1 mul.108
  218.1 0.8 fusion.17
  219.0 0.8 pad_maximum_fusion.2
  219.7 1.9 collective-permute-start.1
  221.7 11.4 %collective-permute-start = (bf16[3,1,160,32]{2,3,1,0:T(8,128)(2,1)S(1)}, bf16[3,1,160,32]{2,3,1,0:T(8,128)(2,1)S(1)}, u32[]{:S(2)}, u32[]{:S(2)}) collective-permute-start(bf16[3,1,160,32]{2,3,1,0:T(8,128)(2,1)S(1)} %pad_maximum_fusion.2), channel_id=1, source_target_pairs={{0,16},{16,32},{32,48},{48,64},{64,80},{80,96},{96,112},{112,128},... | collective-permute-start | bytes 92168 | tf_op jit(solution)/shard_map/ppermute | solution.py:19
  233.1 0.1 collective-permute-done.1
  233.2 2.5 collective-permute-done
  235.7 0.9 select_maximum_fusion
  236.6 0.1 constant_dynamic-update-slice_fusion.24
  236.7 0.7 constant_dynamic-update-slice_fusion.22
  237.6 0.7 constant_dynamic-update-slice_fusion.13
  238.6 0.1 constant_dynamic-update-slice_fusion.4
  238.7 0.1 constant_dynamic-update-slice_fusion.3
  238.9 0.4 convolution_bitcast_fusion
  239.3 1.0 copy.154
  240.4 0.8 copy.152
  241.1 2.0 reshape.194
  243.2 106.8 %reduce-scatter.4.cloned.1.call-done = f32[32,160]{1,0:T(8,128)} async-done(((f32[512,160]{1,0:T(8,128)}), f32[32,160]{1,0:T(8,128)}) %reduce-scatter.4.cloned.1.call-update) | async-done | bytes 20496 | tf_op jit(solution)/shard_map/reduce_scatter | solution.py:79
  350.0 0.9 convert_reduce_fusion.1
  350.9 0.1 reduce_sum.59
  351.0 0.1 reduce_sum.72
  351.1 0.2 dynamic_update_slice.6
  351.4 270.6 %psum.30 = f32[32]{0:T(128)S(1)} all-reduce(f32[32]{0:T(128)S(1)} %dynamic_update_slice.6), channel_id=1, replica_groups=mesh['space'=32,'chan'=16] {'space','chan'}, use_global_device_ids=true, to_apply=%region_9.10 | all-reduce | flops 32 | bytes 256 | tf_op jit(solution)/shard_map/psum | solution.py:98
  622.1 0.1 sub.64
  622.2 0.2 fusion.19
  622.4 0.1 reduce_sum.74
  622.5 0.1 reduce_sum.75
  622.6 0.2 dynamic_update_slice.7
  622.8 100.2 %psum.31 = f32[32]{0:T(128)S(1)} all-reduce(f32[32]{0:T(128)S(1)} %dynamic_update_slice.7), channel_id=1, replica_groups=mesh['space'=32,'chan'=16] {'space','chan'}, use_global_device_ids=true, to_apply=%region_12.13 | all-reduce | flops 32 | bytes 256 | tf_op jit(solution)/shard_map/psum | solution.py:102
  723.0 0.1 copy.124
  723.1 0.5 broadcast.171
  723.6 0.9 reduce.10
  724.5 0.7 reshape.200
  725.2 14.1 %all-to-all-start = ((bf16[16,2,160]{2,1,0:T(2,128)(2,1)}), bf16[16,2,160]{2,1,0:T(2,128)(2,1)S(1)}, u32[]{:S(2)}, u32[]{:S(2)}) async-start(bf16[16,2,160]{2,1,0:T(2,128)(2,1)} %reshape.200), calls=%async_computation | async-start | bytes 32768 | tf_op jit(solution)/shard_map/all_to_all | solution.py:107
  739.4 0.1 mul.116
  739.6 0.1 sub.60
  739.7 4.4 all-to-all-done
  744.1 0.1 reshape.201
  744.2 0.1 convert_bitcast_fusion
  744.3 0.1 reshape.196
  744.5 0.1 fusion.6
  744.6 0.2 slice_maximum_fusion
  744.9 5.9 collective-permute-start.2
  750.8 1.9 collective-permute-start.3
  752.8 1.6 collective-permute-done.2
  754.4 10.8 %collective-permute-done.3 = bf16[3,1,20,512]{3,1,2,0:T(2,128)(2,1)S(1)} collective-permute-done((bf16[3,1,20,512]{3,1,2,0:T(2,128)(2,1)S(1)}, bf16[3,1,20,512]{3,1,2,0:T(2,128)(2,1)S(1)}, u32[]{:S(2)}, u32[]{:S(2)}) %collective-permute-start.3) | collective-permute-done | bytes 61472 | tf_op jit(solution)/shard_map/ppermute | solution.py:21
  765.3 10.6 %collective-permute-start.5 = (bf16[3,4,1,512]{3,1,2,0:T(4,128)(2,1)S(1)}, bf16[3,4,1,512]{3,1,2,0:T(4,128)(2,1)S(1)}, u32[]{:S(2)}, u32[]{:S(2)}) collective-permute-start(bf16[3,4,1,512]{3,1,2,0:T(4,128)(2,1)S(1)} %get-tuple-element.9), channel_id=1, source_target_pairs={{1,0},{2,1},{3,2},{4,3},{5,4},{6,5},{7,6},{8,7},{9,8},{10,9},{11,1... | collective-permute-start | bytes 36872 | tf_op jit(solution)/shard_map/ppermute | solution.py:21
  775.9 1.9 collective-permute-start.4
  777.8 0.6 pad_maximum_fusion.3
  778.7 11.0 %collective-permute-done.4 = bf16[3,4,1,512]{3,1,2,0:T(4,128)(2,1)S(1)} collective-permute-done((bf16[3,4,1,512]{3,1,2,0:T(4,128)(2,1)S(1)}, bf16[3,4,1,512]{3,1,2,0:T(4,128)(2,1)S(1)}, u32[]{:S(2)}, u32[]{:S(2)}) %collective-permute-start.4) | collective-permute-done | bytes 12320 | tf_op jit(solution)/shard_map/ppermute | solution.py:19
  789.6 0.7 pad_maximum_fusion
  790.4 0.5 fusion.23
  792.0 0.3 copy-done.6
  792.3 9.2 %fusion = bf16[40,512]{1,0:T(8,128)(2,1)S(1)} fusion(bf16[40,13824]{1,0:T(8,128)(2,1)S(1)} %constant_dynamic-update-slice_fusion.27, bf16[13824,512]{0,1:T(8,128)(2,1)} %all-gather.2.cloned.1.call-done, f32[512]{0:T(512)S(1)} %copy-done.6), kind=kOutput, calls=%fused_computation.2 | convolution fusion | flops 566272000 | bytes 15304704 | tf_op jit(solution)/shard_map/dot_general | solution.py:118
  801.5 0.6 copy.153
  (147 shorter events, 2.2 us)
Async XLA Ops:
  6.5 232.4 %copy-start = (bf16[3,3,3,32,512]{4,3,2,1,0:T(8,128)(2,1)S(1)}, bf16[3,3,3,32,512]{4,3,2,1,0:T(8,128)(2,1)}, u32[]{:S(2)}) copy-start(bf16[3,3,3,32,512]{4,3,2,1,0:T(8,128)(2,1)} %param.15) | copy-start | bytes 2654212
  6.5 232.1 %copy-start.3 = (bf16[1,1,160,32]{2,3,1,0:T(8,128)(2,1)S(1)}, bf16[1,1,160,32]{2,3,1,0:T(8,128)(2,1)}, u32[]{:S(2)}) copy-start(bf16[1,1,160,32]{2,3,1,0:T(8,128)(2,1)} %param.11) | copy-start | bytes 30724
  6.5 232.1 %copy-start.7 = (f32[32]{0:T(128)S(1)}, f32[32]{0:T(128)}, u32[]{:S(2)}) copy-start(f32[32]{0:T(128)} %param.14) | copy-start | bytes 388
  6.5 232.1 %copy-start.8 = (f32[32]{0:T(128)S(1)}, f32[32]{0:T(128)}, u32[]{:S(2)}) copy-start(f32[32]{0:T(128)} %param.13) | copy-start | bytes 388
  6.5 343.4 %reduce-scatter.4.cloned.1.call-start = ((), (), s32[]{:S(2)}) async-start(), calls=%async_computation.3 | async-start | bytes 557056 | tf_op jit(solution)/shard_map/reduce_scatter | solution.py:79
  219.7 13.5 %collective-permute-start.1 = (bf16[3,1,160,32]{2,3,1,0:T(8,128)(2,1)S(1)}, bf16[3,1,160,32]{2,3,1,0:T(8,128)(2,1)S(1)}, u32[]{:S(2)}, u32[]{:S(2)}) collective-permute-start(bf16[3,1,160,32]{2,3,1,0:T(8,128)(2,1)S(1)} %pad_maximum_fusion.2), channel_id=1, source_target_pairs={{16,0},{32,16},{48,32},{64,48},{80,64},{96,80},{112,96},{128,112},... | collective-permute-start | bytes 92168 | tf_op jit(solution)/shard_map/ppermute | solution.py:21
  221.7 14.0 %collective-permute-start = (bf16[3,1,160,32]{2,3,1,0:T(8,128)(2,1)S(1)}, bf16[3,1,160,32]{2,3,1,0:T(8,128)(2,1)S(1)}, u32[]{:S(2)}, u32[]{:S(2)}) collective-permute-start(bf16[3,1,160,32]{2,3,1,0:T(8,128)(2,1)S(1)} %pad_maximum_fusion.2), channel_id=1, source_target_pairs={{0,16},{16,32},{32,48},{48,64},{64,80},{80,96},{96,112},{112,128},... | collective-permute-start | bytes 92168 | tf_op jit(solution)/shard_map/ppermute | solution.py:19
  238.9 1.5 copy-start.2
  240.3 551.7 %all-gather.2.cloned.1.call-start = ((), (), s32[]{:S(2)}) async-start(), calls=%async_computation.2 | async-start | bytes 15040512 | tf_op jit(solution)/shard_map/all_gather | solution.py:120
  241.1 108.9 %copy-start.9 = (f32[32]{0:T(128)S(1)}, f32[32]{0:T(128)}, u32[]{:S(2)}) copy-start(f32[32]{0:T(128)} %param.16) | copy-start | bytes 388
  243.2 501.3 %copy-start.4 = (f32[512]{0:T(512)S(1)}, f32[512]{0:T(512)}, u32[]{:S(2)}) copy-start(f32[512]{0:T(512)} %param.19) | copy-start | bytes 6148
  243.2 501.3 %copy-start.5 = (f32[512]{0:T(512)S(1)}, f32[512]{0:T(512)}, u32[]{:S(2)}) copy-start(f32[512]{0:T(512)} %param.18) | copy-start | bytes 6148
  243.2 501.5 %copy-start.1 = (bf16[2,2,20,512]{3,1,2,0:T(2,128)(2,1)S(1)}, bf16[2,2,20,512]{3,1,2,0:T(2,128)(2,1)}, u32[]{:S(2)}) copy-start(bf16[2,2,20,512]{3,1,2,0:T(2,128)(2,1)} %param.17) | copy-start | bytes 245764
  243.2 509.5 %slice-start = ((bf16[2,2,20,512]{3,1,2,0:T(2,128)(2,1)}), bf16[1,2,20,512]{3,1,2,0:T(2,128)(2,1)S(1)}, s32[]{:S(2)}) async-start(bf16[2,2,20,512]{3,1,2,0:T(2,128)(2,1)} %param.17), calls=%async_computation.4 | async-start | bytes 81920 | tf_op jit(solution)/shard_map/slice | solution.py:34
  725.2 18.9 %all-to-all-start = ((bf16[16,2,160]{2,1,0:T(2,128)(2,1)}), bf16[16,2,160]{2,1,0:T(2,128)(2,1)S(1)}, u32[]{:S(2)}, u32[]{:S(2)}) async-start(bf16[16,2,160]{2,1,0:T(2,128)(2,1)} %reshape.200), calls=%async_computation | async-start | bytes 32768 | tf_op jit(solution)/shard_map/all_to_all | solution.py:107
  744.9 9.5 %collective-permute-start.2 = (bf16[3,1,20,512]{3,1,2,0:T(2,128)(2,1)S(1)}, bf16[3,1,20,512]{3,1,2,0:T(2,128)(2,1)S(1)}, u32[]{:S(2)}, u32[]{:S(2)}) collective-permute-start(bf16[3,1,20,512]{3,1,2,0:T(2,128)(2,1)S(1)} %get-tuple-element.38), channel_id=1, source_target_pairs={{0,16},{16,32},{32,48},{48,64},{64,80},{80,96},{96,112},{112,128},... | collective-permute-start | bytes 184328 | tf_op jit(solution)/shard_map/ppermute | solution.py:19
  750.8 14.5 %collective-permute-start.3 = (bf16[3,1,20,512]{3,1,2,0:T(2,128)(2,1)S(1)}, bf16[3,1,20,512]{3,1,2,0:T(2,128)(2,1)S(1)}, u32[]{:S(2)}, u32[]{:S(2)}) collective-permute-start(bf16[3,1,20,512]{3,1,2,0:T(2,128)(2,1)S(1)} %get-tuple-element.39), channel_id=1, source_target_pairs={{16,0},{32,16},{48,32},{64,48},{80,64},{96,80},{112,96},{128,112},... | collective-permute-start | bytes 184328 | tf_op jit(solution)/shard_map/ppermute | solution.py:21
  765.3 13.4 %collective-permute-start.5 = (bf16[3,4,1,512]{3,1,2,0:T(4,128)(2,1)S(1)}, bf16[3,4,1,512]{3,1,2,0:T(4,128)(2,1)S(1)}, u32[]{:S(2)}, u32[]{:S(2)}) collective-permute-start(bf16[3,4,1,512]{3,1,2,0:T(4,128)(2,1)S(1)} %get-tuple-element.9), channel_id=1, source_target_pairs={{1,0},{2,1},{3,2},{4,3},{5,4},{6,5},{7,6},{8,7},{9,8},{10,9},{11,1... | collective-permute-start | bytes 36872 | tf_op jit(solution)/shard_map/ppermute | solution.py:21
  775.9 13.7 %collective-permute-start.4 = (bf16[3,4,1,512]{3,1,2,0:T(4,128)(2,1)S(1)}, bf16[3,4,1,512]{3,1,2,0:T(4,128)(2,1)S(1)}, u32[]{:S(2)}, u32[]{:S(2)}) collective-permute-start(bf16[3,4,1,512]{3,1,2,0:T(4,128)(2,1)S(1)} %get-tuple-element.10), channel_id=1, source_target_pairs={{0,1},{1,2},{2,3},{3,4},{4,5},{5,6},{6,7},{7,8},{8,9},{9,10},{10,1... | collective-permute-start | bytes 36872 | tf_op jit(solution)/shard_map/ppermute | solution.py:19
  791.6 0.7 copy-start.6
Sparse Core Ops, SparseCore 0:
  240.4 109.5 reduce-scatter.3
  353.3 250.6 all-gather.1
where the time goes:
time: 810 us; the launch traced here: 809 us
  blocking collectives  580 us (72%)
  waiting for transfers between devices  137 us (17%)
  starting transfers between devices  47.9 us (6%)
  between operations  14.4 us (2%)
  local copies, waits for them, and re-layouts  11.5 us (1%)
  matrix products  9.58 us (1%)
  other arithmetic  8.67 us (1%)
    psum x1, blocking collectives, on_device(): up_mean = lax.psum(place(own_sum), ('space', 'chan')) / entries  271 us
    reduce_scatter x1, waiting for transfers between devices, on_device(): lax.psum_scatter(lax.dot_general(kernel, columns, (((0,), (1,)), ((), ())...  107 us
    psum x1, blocking collectives, on_device(): lax.psum(jnp.sum(centred * centred, axis=(0, 1, 2, 4)), 'space') / entries  106 us
    psum x1, blocking collectives, on_device(): lax.psum(jnp.sum(grouped, axis=(0, 1, 2, 4)), 'space') / entries  103 us
    psum x1, blocking collectives, on_device(): lax.psum(place(jnp.sum(deviation * deviation, axis=(0, 1, 2, 4))), ('spac...  100 us
    ppermute x3, starting transfers between devices, extended(): lax.ppermute(tail, axis, [(i, (i + 1) % count) for i in range(ends)])  19.2 us
  transfers between devices with their start and end apart: 9, of which 7 were waited for; matrix products, arithmetic and copies ran while one was open for 1% of the time, Pallas kernels for 0%

commit v1 on v0

--- a/solution.py
+++ b/solution.py
@@ -64,7 +64,8 @@
     values = latent.astype(jnp.float32)
     grouped = values.reshape(frames, height, breadth, groups_here, GS)
     entries = frames * height * lax.axis_size("space") * breadth * GS
-    group_mean = lax.psum(jnp.sum(grouped, axis=(0, 1, 2, 4)), "space") / entries
+    convert_ladders = lambda mat, axis_tag: jnp.sum(lax.all_gather(mat, axis_tag), 0)
+    group_mean = convert_ladders(jnp.sum(grouped, axis=(0, 1, 2, 4)), "space") / entries
     centred = grouped - group_mean[:, None]
     group_var = lax.psum(jnp.sum(centred * centred, axis=(0, 1, 2, 4)), "space") / entries
     scaled = (centred * lax.rsqrt(group_var + epsilon)[:, None]).reshape(

time: 810 us -> 812 us (level)
    psum x1 -> x0, blocking collectives: 103 us -> none  [on_device(): lax.psum(jnp.sum(grouped, axis=(0, 1, 2, 4)), 'space') / entries]
    unnamed x0 -> x1, blocking collectives: none -> 103 us
where the time goes in v1:
time: 812 us; the launch traced here: 811 us
  blocking collectives  580 us (71%)
  waiting for transfers between devices  137 us (17%)
  starting transfers between devices  48 us (6%)
  between operations  15.1 us (2%)
  local copies, waits for them, and re-layouts  13.1 us (2%)
  matrix products  9.59 us (1%)
  other arithmetic  8.7 us (1%)
    psum x1, blocking collectives, on_device(): up_mean = lax.psum(place(own_sum), ('space', 'chan')) / entries  270 us
    reduce_scatter x1, waiting for transfers between devices, on_device(): lax.psum_scatter(lax.dot_general(kernel, columns, (((0,), (1,)), ((), ())...  107 us
    psum x1, blocking collectives, on_device(): lax.psum(jnp.sum(centred * centred, axis=(0, 1, 2, 4)), 'space') / entries  106 us
    unnamed x1, blocking collectives  103 us
    psum x1, blocking collectives, on_device(): lax.psum(place(jnp.sum(deviation * deviation, axis=(0, 1, 2, 4))), ('spac...  100 us
    ppermute x3, starting transfers between devices, extended(): lax.ppermute(tail, axis, [(i, (i + 1) % count) for i in range(ends)])  19.3 us
  transfers between devices with their start and end apart: 9, of which 7 were waited for; matrix products, arithmetic and copies ran while one was open for 1% of the time, Pallas kernels for 0%

profile of v1, /device:TPU:480, one launch (start us, length us, event | category | flops | bytes accessed | tf_op | source)
XLA Modules:
  0.0 811.3 jit_solution(13656464217806238048)
XLA Ops:
  6.6 0.9 convert_reduce_fusion
  7.5 0.1 reduce_sum.58
  7.6 1.3 dynamic-slice
  9.5 0.1 reduce_sum.59
  9.6 0.2 dynamic-update-slice
  9.9 103.2 %all-reduce.1 = f32[64]{0:T(128)S(1)} all-reduce(f32[64]{0:T(128)S(1)} %dynamic-update-slice), channel_id=2, replica_groups=mesh['space'=32,'chan'=16] {'space'}, use_global_device_ids=true, to_apply=%add.1 | all-reduce | flops 64 | bytes 512
  113.0 0.1 reshape.200
  113.2 0.1 sub.57
  113.3 0.9 fusion.9
  114.2 0.1 reduce_sum.62
  114.3 0.1 reduce_sum.66
  114.4 105.8 %psum.21 = f32[2]{0:T(128)S(1)} all-reduce(f32[2]{0:T(128)S(1)} %reduce_sum.66), channel_id=1, replica_groups=mesh['space'=32,'chan'=16] {'space'}, use_global_device_ids=true, to_apply=%region_5.6 | all-reduce | flops 2 | bytes 16 | tf_op jit(solution)/shard_map/psum | solution.py:70
  220.3 0.1 mul.108
  220.4 0.8 fusion.17
  221.2 0.8 pad_maximum_fusion.2
  222.0 1.9 collective-permute-start.1
  223.9 11.4 %collective-permute-start = (bf16[3,1,160,32]{2,3,1,0:T(8,128)(2,1)S(1)}, bf16[3,1,160,32]{2,3,1,0:T(8,128)(2,1)S(1)}, u32[]{:S(2)}, u32[]{:S(2)}) collective-permute-start(bf16[3,1,160,32]{2,3,1,0:T(8,128)(2,1)S(1)} %pad_maximum_fusion.2), channel_id=1, source_target_pairs={{0,16},{16,32},{32,48},{48,64},{64,80},{80,96},{96,112},{112,128},... | collective-permute-start | bytes 92168 | tf_op jit(solution)/shard_map/ppermute | solution.py:19
  235.4 0.1 collective-permute-done.1
  235.5 2.5 collective-permute-done
  238.0 0.9 select_maximum_fusion
  239.0 0.7 constant_dynamic-update-slice_fusion.22
  240.0 0.7 constant_dynamic-update-slice_fusion.13
  240.9 0.1 constant_dynamic-update-slice_fusion.4
  241.2 0.4 convolution_bitcast_fusion
  241.6 1.0 copy.154
  242.7 0.8 copy.152
  243.5 2.0 reshape.196
  245.5 106.8 %reduce-scatter.4.cloned.1.call-done = f32[32,160]{1,0:T(8,128)} async-done(((f32[512,160]{1,0:T(8,128)}), f32[32,160]{1,0:T(8,128)}) %reduce-scatter.4.cloned.1.call-update) | async-done | bytes 20496 | tf_op jit(solution)/shard_map/reduce_scatter | solution.py:80
  352.3 0.9 convert_reduce_fusion.1
  353.3 0.1 reduce_sum.81
  353.3 0.1 reduce_sum.82
  353.5 0.2 dynamic_update_slice.6
  353.7 270.5 %psum.22 = f32[32]{0:T(128)S(1)} all-reduce(f32[32]{0:T(128)S(1)} %dynamic_update_slice.6), channel_id=1, replica_groups=mesh['space'=32,'chan'=16] {'space','chan'}, use_global_device_ids=true, to_apply=%region_9.10 | all-reduce | flops 32 | bytes 256 | tf_op jit(solution)/shard_map/psum | solution.py:99
  624.4 0.1 sub.64
  624.4 0.2 fusion.19
  624.6 0.1 reduce_sum.84
  624.7 0.1 reduce_sum.85
  624.8 0.2 dynamic_update_slice.7
  625.1 100.3 %psum.23 = f32[32]{0:T(128)S(1)} all-reduce(f32[32]{0:T(128)S(1)} %dynamic_update_slice.7), channel_id=1, replica_groups=mesh['space'=32,'chan'=16] {'space','chan'}, use_global_device_ids=true, to_apply=%region_12.13 | all-reduce | flops 32 | bytes 256 | tf_op jit(solution)/shard_map/psum | solution.py:103
  725.4 0.1 copy.124
  725.5 0.5 broadcast.175
  726.0 0.9 reduce.10
  726.9 0.7 reshape.208
  727.6 14.1 %all-to-all-start = ((bf16[16,2,160]{2,1,0:T(2,128)(2,1)}), bf16[16,2,160]{2,1,0:T(2,128)(2,1)S(1)}, u32[]{:S(2)}, u32[]{:S(2)}) async-start(bf16[16,2,160]{2,1,0:T(2,128)(2,1)} %reshape.208), calls=%async_computation | async-start | bytes 32768 | tf_op jit(solution)/shard_map/all_to_all | solution.py:108
  741.8 0.1 mul.116
  742.1 4.4 all-to-all-done
  746.5 0.1 reshape.209
  746.6 0.1 convert_bitcast_fusion
  746.7 0.1 reshape.198
  746.9 0.1 fusion.6
  747.0 0.2 slice_maximum_fusion
  747.2 5.8 collective-permute-start.2
  753.0 1.9 collective-permute-start.3
  755.1 1.6 collective-permute-done.2
  756.7 10.8 %collective-permute-done.3 = bf16[3,1,20,512]{3,1,2,0:T(2,128)(2,1)S(1)} collective-permute-done((bf16[3,1,20,512]{3,1,2,0:T(2,128)(2,1)S(1)}, bf16[3,1,20,512]{3,1,2,0:T(2,128)(2,1)S(1)}, u32[]{:S(2)}, u32[]{:S(2)}) %collective-permute-start.3) | collective-permute-done | bytes 61472 | tf_op jit(solution)/shard_map/ppermute | solution.py:21
  767.5 10.6 %collective-permute-start.5 = (bf16[3,4,1,512]{3,1,2,0:T(4,128)(2,1)S(1)}, bf16[3,4,1,512]{3,1,2,0:T(4,128)(2,1)S(1)}, u32[]{:S(2)}, u32[]{:S(2)}) collective-permute-start(bf16[3,4,1,512]{3,1,2,0:T(4,128)(2,1)S(1)} %get-tuple-element.9), channel_id=1, source_target_pairs={{1,0},{2,1},{3,2},{4,3},{5,4},{6,5},{7,6},{8,7},{9,8},{10,9},{11,1... | collective-permute-start | bytes 36872 | tf_op jit(solution)/shard_map/ppermute | solution.py:21
  778.2 2.1 collective-permute-start.4
  780.3 0.6 pad_maximum_fusion.3
  781.1 10.8 %collective-permute-done.4 = bf16[3,4,1,512]{3,1,2,0:T(4,128)(2,1)S(1)} collective-permute-done((bf16[3,4,1,512]{3,1,2,0:T(4,128)(2,1)S(1)}, bf16[3,4,1,512]{3,1,2,0:T(4,128)(2,1)S(1)}, u32[]{:S(2)}, u32[]{:S(2)}) %collective-permute-start.4) | collective-permute-done | bytes 12320 | tf_op jit(solution)/shard_map/ppermute | solution.py:19
  791.9 0.7 pad_maximum_fusion
  792.6 0.5 fusion.23
  794.3 0.3 copy-done.6
  794.5 9.2 %fusion = bf16[40,512]{1,0:T(8,128)(2,1)S(1)} fusion(bf16[40,13824]{1,0:T(8,128)(2,1)S(1)} %constant_dynamic-update-slice_fusion.27, bf16[13824,512]{0,1:T(8,128)(2,1)} %all-gather.3.cloned.1.call-done, f32[512]{0:T(512)S(1)} %copy-done.6), kind=kOutput, calls=%fused_computation.2 | convolution fusion | flops 566272000 | bytes 15304704 | tf_op jit(solution)/shard_map/dot_general | solution.py:119
  803.8 0.6 copy.153
  (152 shorter events, 2.4 us)
Async XLA Ops:
  6.5 234.7 %copy-start = (bf16[3,3,3,32,512]{4,3,2,1,0:T(8,128)(2,1)S(1)}, bf16[3,3,3,32,512]{4,3,2,1,0:T(8,128)(2,1)}, u32[]{:S(2)}) copy-start(bf16[3,3,3,32,512]{4,3,2,1,0:T(8,128)(2,1)} %param.15) | copy-start | bytes 2654212
  6.5 234.4 %copy-start.3 = (bf16[1,1,160,32]{2,3,1,0:T(8,128)(2,1)S(1)}, bf16[1,1,160,32]{2,3,1,0:T(8,128)(2,1)}, u32[]{:S(2)}) copy-start(bf16[1,1,160,32]{2,3,1,0:T(8,128)(2,1)} %param.11) | copy-start | bytes 30724
  6.5 234.4 %copy-start.7 = (f32[32]{0:T(128)S(1)}, f32[32]{0:T(128)}, u32[]{:S(2)}) copy-start(f32[32]{0:T(128)} %param.14) | copy-start | bytes 388
  6.5 234.4 %copy-start.8 = (f32[32]{0:T(128)S(1)}, f32[32]{0:T(128)}, u32[]{:S(2)}) copy-start(f32[32]{0:T(128)} %param.13) | copy-start | bytes 388
  6.5 345.8 %reduce-scatter.4.cloned.1.call-start = ((), (), s32[]{:S(2)}) async-start(), calls=%async_computation.3 | async-start | bytes 557056 | tf_op jit(solution)/shard_map/reduce_scatter | solution.py:80
  222.0 13.5 %collective-permute-start.1 = (bf16[3,1,160,32]{2,3,1,0:T(8,128)(2,1)S(1)}, bf16[3,1,160,32]{2,3,1,0:T(8,128)(2,1)S(1)}, u32[]{:S(2)}, u32[]{:S(2)}) collective-permute-start(bf16[3,1,160,32]{2,3,1,0:T(8,128)(2,1)S(1)} %pad_maximum_fusion.2), channel_id=1, source_target_pairs={{16,0},{32,16},{48,32},{64,48},{80,64},{96,80},{112,96},{128,112},... | collective-permute-start | bytes 92168 | tf_op jit(solution)/shard_map/ppermute | solution.py:21
  223.9 14.1 %collective-permute-start = (bf16[3,1,160,32]{2,3,1,0:T(8,128)(2,1)S(1)}, bf16[3,1,160,32]{2,3,1,0:T(8,128)(2,1)S(1)}, u32[]{:S(2)}, u32[]{:S(2)}) collective-permute-start(bf16[3,1,160,32]{2,3,1,0:T(8,128)(2,1)S(1)} %pad_maximum_fusion.2), channel_id=1, source_target_pairs={{0,16},{16,32},{32,48},{48,64},{64,80},{80,96},{96,112},{112,128},... | collective-permute-start | bytes 92168 | tf_op jit(solution)/shard_map/ppermute | solution.py:19
  241.2 1.5 copy-start.2
  242.6 551.6 %all-gather.3.cloned.1.call-start = ((), (), s32[]{:S(2)}) async-start(), calls=%async_computation.2 | async-start | bytes 15040512 | tf_op jit(solution)/shard_map/all_gather | solution.py:121
  243.4 108.9 %copy-start.9 = (f32[32]{0:T(128)S(1)}, f32[32]{0:T(128)}, u32[]{:S(2)}) copy-start(f32[32]{0:T(128)} %param.16) | copy-start | bytes 388
  245.5 501.4 %copy-start.4 = (f32[512]{0:T(512)S(1)}, f32[512]{0:T(512)}, u32[]{:S(2)}) copy-start(f32[512]{0:T(512)} %param.19) | copy-start | bytes 6148
  245.5 501.4 %copy-start.5 = (f32[512]{0:T(512)S(1)}, f32[512]{0:T(512)}, u32[]{:S(2)}) copy-start(f32[512]{0:T(512)} %param.18) | copy-start | bytes 6148
  245.5 501.5 %copy-start.1 = (bf16[2,2,20,512]{3,1,2,0:T(2,128)(2,1)S(1)}, bf16[2,2,20,512]{3,1,2,0:T(2,128)(2,1)}, u32[]{:S(2)}) copy-start(bf16[2,2,20,512]{3,1,2,0:T(2,128)(2,1)} %param.17) | copy-start | bytes 245764
  245.5 509.4 %slice-start = ((bf16[2,2,20,512]{3,1,2,0:T(2,128)(2,1)}), bf16[1,2,20,512]{3,1,2,0:T(2,128)(2,1)S(1)}, s32[]{:S(2)}) async-start(bf16[2,2,20,512]{3,1,2,0:T(2,128)(2,1)} %param.17), calls=%async_computation.4 | async-start | bytes 81920 | tf_op jit(solution)/shard_map/slice | solution.py:34
  727.6 18.9 %all-to-all-start = ((bf16[16,2,160]{2,1,0:T(2,128)(2,1)}), bf16[16,2,160]{2,1,0:T(2,128)(2,1)S(1)}, u32[]{:S(2)}, u32[]{:S(2)}) async-start(bf16[16,2,160]{2,1,0:T(2,128)(2,1)} %reshape.208), calls=%async_computation | async-start | bytes 32768 | tf_op jit(solution)/shard_map/all_to_all | solution.py:108
  747.2 9.4 %collective-permute-start.2 = (bf16[3,1,20,512]{3,1,2,0:T(2,128)(2,1)S(1)}, bf16[3,1,20,512]{3,1,2,0:T(2,128)(2,1)S(1)}, u32[]{:S(2)}, u32[]{:S(2)}) collective-permute-start(bf16[3,1,20,512]{3,1,2,0:T(2,128)(2,1)S(1)} %get-tuple-element.38), channel_id=1, source_target_pairs={{0,16},{16,32},{32,48},{48,64},{64,80},{80,96},{96,112},{112,128},... | collective-permute-start | bytes 184328 | tf_op jit(solution)/shard_map/ppermute | solution.py:19
  753.0 14.5 %collective-permute-start.3 = (bf16[3,1,20,512]{3,1,2,0:T(2,128)(2,1)S(1)}, bf16[3,1,20,512]{3,1,2,0:T(2,128)(2,1)S(1)}, u32[]{:S(2)}, u32[]{:S(2)}) collective-permute-start(bf16[3,1,20,512]{3,1,2,0:T(2,128)(2,1)S(1)} %get-tuple-element.39), channel_id=1, source_target_pairs={{16,0},{32,16},{48,32},{64,48},{80,64},{96,80},{112,96},{128,112},... | collective-permute-start | bytes 184328 | tf_op jit(solution)/shard_map/ppermute | solution.py:21
  767.5 13.6 %collective-permute-start.5 = (bf16[3,4,1,512]{3,1,2,0:T(4,128)(2,1)S(1)}, bf16[3,4,1,512]{3,1,2,0:T(4,128)(2,1)S(1)}, u32[]{:S(2)}, u32[]{:S(2)}) collective-permute-start(bf16[3,4,1,512]{3,1,2,0:T(4,128)(2,1)S(1)} %get-tuple-element.9), channel_id=1, source_target_pairs={{1,0},{2,1},{3,2},{4,3},{5,4},{6,5},{7,6},{8,7},{9,8},{10,9},{11,1... | collective-permute-start | bytes 36872 | tf_op jit(solution)/shard_map/ppermute | solution.py:21
  778.2 13.7 %collective-permute-start.4 = (bf16[3,4,1,512]{3,1,2,0:T(4,128)(2,1)S(1)}, bf16[3,4,1,512]{3,1,2,0:T(4,128)(2,1)S(1)}, u32[]{:S(2)}, u32[]{:S(2)}) collective-permute-start(bf16[3,4,1,512]{3,1,2,0:T(4,128)(2,1)S(1)} %get-tuple-element.10), channel_id=1, source_target_pairs={{0,1},{1,2},{2,3},{3,4},{4,5},{5,6},{6,7},{7,8},{8,9},{9,10},{10,1... | collective-permute-start | bytes 36872 | tf_op jit(solution)/shard_map/ppermute | solution.py:19
  793.9 0.7 copy-start.6
Sparse Core Ops, SparseCore 0:
  242.7 109.5 reduce-scatter.3
  355.6 250.0 all-gather.2
